TPU v7x, 32 devices: a whole 2x2x4 slice. The times are simulated.
32 devices in a mesh: tm: 2 (over x), diamond: 2 (over y), tile: 8 (over z, core).
Axes of the slice: x: 2, y: 2, z: 4, core: 2. Of those that a mesh axis runs over, the one named last changes fastest.
Arguments:
- activations: bfloat16 [8, 2, 32, 64, 256], P('tm', 'diamond', 'tile'), may hold values from -6 to 6
- upstream: bfloat16 [8, 2, 32, 64, 256], P('tm', 'diamond', 'tile'), may hold values from -16 to 16
- hex_weight: bfloat16 [7, 64, 64], replicated, may hold values from -0.25 to 0.25
- time_weight: bfloat16 [3, 64, 64], replicated, may hold values from -0.4375 to 0.4375
- left_map: int32 [2, 32], replicated, may hold values from 0 to 31, each once within a row
- right_map: int32 [2, 32], replicated, may hold values from 0 to 31, each once within a row
Outputs:
- grad_input: bfloat16 [8, 2, 32, 64, 256], P('tm', 'diamond', 'tile')
- grad_hex: float32 [7, 64, 64], replicated
- grad_time: float32 [3, 64, 64], replicated
Inputs may be any that keep to these rules, and one draw needn't show every extreme that they name: Each row of left_map holds every number of 0 to 31 once. Each row of right_map holds every number of 0 to 31 once.
All inputs are finite; a program needn't handle non-finite values.
Results may differ from a plain program's by a relative error of at most 0.0035.
Values may be sent and summed in bfloat16 or wider, within the bound.
A program may use at most 64 MiB of HBM per device.

v0:
```python
import jax
import jax.numpy as jnp
from jax import lax
from jax.sharding import PartitionSpec as P

OFFSETS = ((0, 0), (0, 1), (0, -1), (1, 0), (-1, 0), (1, -1), (-1, 1))


def from_behind(block, axis, distance):
    devices = range(lax.axis_size(axis))
    route = [((i - distance) % len(devices), i) for i in devices]
    return lax.ppermute(block, axis, route)


def with_halo(x, sides, width):
    for axis, dim in sides:
        size, length = (lax.axis_size(axis), x.shape[dim])
        up = [(i, (i + 1) % size) for i in range(size - 1)]
        down = [(j, i) for i, j in up]
        last = lax.slice_in_dim(x, length - width, length, axis=dim)
        initial = lax.slice_in_dim(x, 0, width, axis=dim)
        before = lax.ppermute(last, axis, up)
        after = lax.ppermute(initial, axis, down)
        x = jnp.concatenate([before, x, after], axis=dim)
    return x


def passed_along(block, axis, distance):
    devices = range(lax.axis_size(axis))
    route = [(i - distance, i) for i in devices if i - distance in devices]
    return lax.ppermute(block, axis, route)


def silu_slope(hidden):
    sigmoid = jax.nn.sigmoid(hidden)
    return sigmoid * (1.0 + hidden * (1.0 - sigmoid))


def shards(activations, upstream, hex_weight, time_weight, left_map, right_map):
    field = activations[:, 0]
    cotangent = upstream[:, 0]
    frames, tile_rows, channels, columns = field.shape
    chart = lax.axis_index("diamond")
    first_row = lax.axis_index("tile") * tile_rows
    chart_rows = tile_rows * lax.axis_size("tile")
    own_left = lax.dynamic_slice(left_map, (chart, first_row), (1, tile_rows))[0]
    own_right = lax.dynamic_slice(right_map, (chart, first_row), (1, tile_rows))[0]
    strips = (
        lax.all_gather(field[..., 0], "tile", axis=1, tiled=True),
        lax.all_gather(field[..., columns - 1], "tile", axis=1, tiled=True),
    )
    prev_right = from_behind(strips[1], "diamond", 1)
    next_left = from_behind(strips[0], "diamond", -1)
    ghost_left = jnp.take(prev_right, own_left, axis=1)
    ghost_right = jnp.take(next_left, own_right, axis=1)
    widened = jnp.concatenate([ghost_left[..., None], field, ghost_right[..., None]], axis=-1)
    depth = 1
    margin = depth - 1
    span_rows = tile_rows + 2 * margin
    padded = with_halo(widened, (("tile", 1),), depth)
    hidden = jnp.zeros((frames, span_rows, channels, columns), jnp.float32)
    for number, (step_row, step_col) in enumerate(OFFSETS):
        window = padded[
            :, 1 + step_row : 1 + step_row + span_rows, :, 1 + step_col : 1 + step_col + columns
        ]
        hidden = hidden + jnp.einsum(
            "frcx,cd->frdx", window, hex_weight[number], preferred_element_type=jnp.float32
        )
    active = jax.nn.silu(hidden).astype(jnp.bfloat16)
    framed = with_halo(cotangent, (("tm", 0),), 1)
    grad_act = jnp.zeros((frames, span_rows, channels, columns), jnp.float32)
    time_terms = []
    for number in range(3):
        shifted = framed[2 - number : 2 - number + frames]
        grad_act = grad_act + jnp.einsum(
            "frdx,cd->frcx", shifted, time_weight[number], preferred_element_type=jnp.float32
        )
        time_terms.append(
            jnp.einsum("frcx,frdx->cd", active, shifted, preferred_element_type=jnp.float32)
        )
    grad_wide = (grad_act * silu_slope(hidden)).astype(jnp.bfloat16)
    hex_terms = []
    for number, (step_row, step_col) in enumerate(OFFSETS):
        begin = 1 + margin + step_row
        window = padded[:, begin : begin + tile_rows, :, 1 + step_col : 1 + step_col + columns]
        hex_terms.append(
            jnp.einsum("frcx,frdx->cd", window, grad_wide, preferred_element_type=jnp.float32)
        )
    spread = jnp.zeros((frames, tile_rows + 2, channels, columns + 2), jnp.float32)
    for number, (step_row, step_col) in enumerate(OFFSETS):
        spread = spread.at[
            :, 1 + step_row : 1 + step_row + tile_rows, :, 1 + step_col : 1 + step_col + columns
        ].add(
            jnp.einsum(
                "frdx,cd->frcx", grad_wide, hex_weight[number], preferred_element_type=jnp.float32
            )
        )
    from_below = passed_along(spread[:, 0].astype(jnp.bfloat16), "tile", -1).astype(jnp.float32)
    from_above = passed_along(spread[:, tile_rows + 1].astype(jnp.bfloat16), "tile", 1).astype(
        jnp.float32
    )
    owned = spread[:, 1 : tile_rows + 1]
    owned = owned.at[:, 0].add(from_above)
    owned = owned.at[:, tile_rows - 1].add(from_below)
    total = cotangent.astype(jnp.float32) + owned[..., 1 : columns + 1]
    left_grad = owned[..., 0]
    right_grad = owned[..., columns + 1]
    strip_left = (
        jnp.zeros((frames, chart_rows, channels), jnp.float32).at[:, own_left].set(left_grad)
    )
    strip_right = (
        jnp.zeros((frames, chart_rows, channels), jnp.float32).at[:, own_right].set(right_grad)
    )
    moved_left = from_behind(strip_left.astype(jnp.bfloat16), "diamond", -1).astype(
        strip_left.dtype
    )
    moved_right = from_behind(strip_right.astype(jnp.bfloat16), "diamond", 1).astype(
        strip_right.dtype
    )
    into_last, into_first = (
        lax.psum_scatter(
            moved_left.astype(jnp.bfloat16), "tile", scatter_dimension=1, tiled=True
        ).astype(jnp.float32),
        lax.psum_scatter(
            moved_right.astype(jnp.bfloat16), "tile", scatter_dimension=1, tiled=True
        ).astype(jnp.float32),
    )
    total = total.at[..., columns - 1].add(into_last)
    total = total.at[..., 0].add(into_first)
    hex_local = jnp.stack(hex_terms)
    time_local = jnp.stack(time_terms)
    grad_hex, grad_time = lax.psum((hex_local, time_local), ("tm", "diamond", "tile"))
    return (total.astype(jnp.bfloat16)[:, None], grad_hex, grad_time)


def solution(mesh):
    in_specs = (
        P("tm", "diamond", "tile", None, None),
        P("tm", "diamond", "tile", None, None),
        P(),
        P(),
        P(),
        P(),
    )
    out_specs = (P("tm", "diamond", "tile", None, None), P(), P())
    return jax.shard_map(shards, mesh=mesh, in_specs=in_specs, out_specs=out_specs, check_vma=False)
```

profile of v0, /device:TPU:0, one launch (start us, length us, event | category | flops | bytes accessed | tf_op | source)
XLA Modules:
  0.0 317.2 jit_solution(10565177064639616680)
XLA Ops:
  7.2 1.2 fusion.91
  8.4 25.1 %all-gather = bf16[4,32,64,1]{3,2,1,0:T(8,128)(2,1)S(1)} all-gather(bf16[4,4,64,1]{3,2,1,0:T(8,128)(2,1)S(1)} %get-tuple-element.164), channel_id=2, replica_groups=mesh['tm'=2,'diamond'=2,'tile'=8] {'tile'}, dimensions={1}, use_global_device_ids=true | all-gather | bytes 18432 | tf_op jit(solution)/shard_map/all_gather | solution.py:49
  33.5 1.1 copy.161
  34.6 1.6 collective-permute-start.2
  36.2 22.7 %all-gather.1 = bf16[4,32,64,1]{3,2,1,0:T(8,128)(2,1)S(1)} all-gather(bf16[4,4,64,1]{3,2,1,0:T(8,128)(2,1)S(1)} %get-tuple-element.163), channel_id=3, replica_groups=mesh['tm'=2,'diamond'=2,'tile'=8] {'tile'}, dimensions={1}, use_global_device_ids=true | all-gather | bytes 18432 | tf_op jit(solution)/shard_map/all_gather | solution.py:50
  58.9 1.1 copy.162
  61.2 4.2 %collective-permute-start.1 = (bf16[1,4,64,256]{3,2,1,0:T(8,128)(2,1)}, bf16[1,4,64,256]{3,2,1,0:T(8,128)(2,1)}, u32[]{:S(2)}, u32[]{:S(2)}) collective-permute-start(bf16[1,4,64,256]{3,2,1,0:T(8,128)(2,1)} %get-tuple-element.162), channel_id=1, source_target_pairs={{0,16},{1,17},{2,18},{3,19},{4,20},{5,21},{6,22},{7,23},{8,24},{9,... | collective-permute-start | bytes 393224 | tf_op jit(solution)/shard_map/ppermute | solution.py:22
  65.4 1.3 collective-permute-start
  66.9 1.0 convolution_bitcast_fusion.16
  69.1 2.7 and_reduce_fusion
  76.3 1.4 collective-permute-start.4
  77.7 3.2 %collective-permute-start.5 = (bf16[4,1,64,258]{3,2,1,0:T(8,128)(2,1)S(1)}, bf16[4,1,64,258]{3,2,1,0:T(8,128)(2,1)S(1)}, u32[]{:S(2)}, u32[]{:S(2)}) collective-permute-start(bf16[4,1,64,258]{3,2,1,0:T(8,128)(2,1)S(1)} %get-tuple-element.160), channel_id=1, source_target_pairs={{0,1},{1,2},{2,3},{3,4},{4,5},{5,6},{6,7},{8,9},{9,10},{10,11},{11... | collective-permute-start | bytes 396296 | tf_op jit(solution)/shard_map/ppermute | solution.py:22
  81.3 1.2 convolution_bitcast_fusion.13
  84.5 1.5 multiply_convert_fusion
  86.0 1.5 fusion.15
  88.7 1.4 fusion.9
  90.5 7.1 %scatter-add.39 = f32[4,6,64,258]{3,2,0,1:T(8,128)S(1)} dynamic-update-slice(f32[4,6,64,258]{3,2,0,1:T(8,128)S(1)} %scatter-add.36, f32[4,4,64,256]{3,2,0,1:T(8,128)} %fusion.9, s32[]{:T(128)} %constant.332.clone.1, s32[]{:T(128)} %constant.338.clone.1, s32[]{:T(128)} %constant.332.clone.1, s32[]{:T(128)} %constant.333.clone.1) | dynamic-update-slice | bytes 2097156 | tf_op jit(solution)/shard_map/scatter-add | solution.py:93
  97.9 1.3 fusion.12
  99.3 7.1 %scatter-add.41 = f32[4,6,64,258]{3,2,0,1:T(8,128)S(1)} dynamic-update-slice(f32[4,6,64,258]{3,2,0,1:T(8,128)S(1)} %fusion.11, f32[4,4,64,256]{3,2,0,1:T(8,128)} %fusion.12, s32[]{:T(128)} %constant.332.clone.1, s32[]{:T(128)} %constant.333.clone.1, s32[]{:T(128)} %constant.332.clone.1, s32[]{:T(128)} %constant.338.clone.1) | dynamic-update-slice | bytes 2097156 | tf_op jit(solution)/shard_map/scatter-add | solution.py:93
  106.3 2.7 add_select_fusion.1
  109.0 7.8 %scatter-add.44 = f32[4,6,64,258]{3,2,0,1:T(8,128)S(1)} dynamic-update-slice(f32[4,6,64,258]{3,2,0,1:T(8,128)S(1)} %scatter-add.41, f32[4,4,64,256]{3,2,0,1:T(8,128)} %add_select_fusion.1, s32[]{:T(128)} %constant.332.clone.1, s32[]{:T(128)S(1)} %bitcast.366, s32[]{:T(128)} %constant.332.clone.1, s32[]{:T(128)} %bitcast.61) | dynamic-update-slice | bytes 2097156 | tf_op jit(solution)/shard_map/scatter-add | solution.py:93
  117.1 3.2 add_select_fusion
  120.3 8.4 %scatter-add.46 = f32[4,6,64,258]{3,2,0,1:T(8,128)S(1)} dynamic-update-slice(f32[4,6,64,258]{3,2,0,1:T(8,128)S(1)} %fusion.14, f32[4,4,64,256]{3,2,0,1:T(8,128)} %add_select_fusion, s32[]{:T(128)} %constant.332.clone.1, s32[]{:T(128)} %bitcast.66, s32[]{:T(128)} %constant.332.clone.1, s32[]{:T(128)} %bitcast.67) | dynamic-update-slice | bytes 2097156 | tf_op jit(solution)/shard_map/scatter-add | solution.py:93
  128.7 1.2 convert.16
  129.9 1.3 slice.528
  131.2 1.0 fusion.21
  132.2 1.0 fusion.20
  133.2 1.0 fusion.19
  134.2 1.0 fusion.18
  135.2 0.9 fusion.17
  136.1 1.0 fusion.16
  137.2 1.4 convolution_bitcast_fusion.18
  138.6 1.8 slice_bitcast_fusion.1
  140.4 4.4 %collective-permute-start.6 = (bf16[4,64,258]{2,1,0:T(8,128)(2,1)}, bf16[4,64,258]{2,1,0:T(8,128)(2,1)}, u32[]{:S(2)}, u32[]{:S(2)}) collective-permute-start(bf16[4,64,258]{2,1,0:T(8,128)(2,1)} %get-tuple-element.156), channel_id=1, source_target_pairs={{0,1},{1,2},{2,3},{3,4},{4,5},{5,6},{6,7},{8,9},{9,10},{10,11},{11... | collective-permute-start | bytes 396296 | tf_op jit(solution)/shard_map/ppermute | solution.py:31
  144.8 1.3 collective-permute-start.7
  146.1 1.3 convolution_bitcast_fusion.17
  147.5 1.2 convolution_bitcast_fusion.19
  148.7 45.7 %psum.15 = f32[3,64,64]{2,1,0:T(8,128)} all-reduce(f32[3,64,64]{2,1,0:T(8,128)S(1)} %pad_maximum_fusion.16), channel_id=1, replica_groups=mesh['tm'=2,'diamond'=2,'tile'=8] {'tm','diamond','tile'}, use_global_device_ids=true, to_apply=%region_7.9 | all-reduce | flops 12288 | bytes 98304 | tf_op jit(solution)/shard_map/psum | solution.py:132
  194.3 71.3 %all-reduce.6.cloned.1.call-done = f32[7,64,64]{1,2,0:T(8,128)} async-done(((f32[7,64,64]{1,2,0:T(8,128)}), f32[7,64,64]{1,2,0:T(8,128)}) %all-reduce.6.cloned.1.call-update) | async-done | bytes 114704 | tf_op jit(solution)/shard_map/psum | solution.py:132
  265.6 1.8 copy.133
  267.4 1.7 fusion.33
  269.1 1.5 copy.119
  270.6 1.1 fusion.32
  273.0 1.5 collective-permute-start.8
  276.1 1.1 collective-permute-done.8
  277.2 1.9 collective-permute-done.9
  279.1 26.9 %all-reduce.3 = (bf16[4,32,64]{2,0,1:T(4,128)(2,1)S(1)}, bf16[4,32,64]{2,0,1:T(4,128)(2,1)S(1)}) all-reduce(bf16[4,32,64]{2,0,1:T(4,128)(2,1)S(1)} %collective-permute-done.8, bf16[4,32,64]{2,0,1:T(4,128)(2,1)S(1)} %collective-permute-done.9), channel_id=4, replica_groups=mesh['tm'=2,'diamond'=2,'tile'=8] {'tile'}, use_global_device_ids=true, to_apply=%region_3.5.clone | all-reduce | flops 16384 | bytes 65536
  306.8 1.9 scatter-add.51
  (100 shorter events, 16.1 us)
Async XLA Ops:
  7.2 258.5 %all-reduce.6.cloned.1.call-start = ((), (), s32[]{:S(2)}) async-start(), calls=%async_computation | async-start | bytes 458752 | tf_op jit(solution)/shard_map/psum | solution.py:132
  34.6 38.7 %collective-permute-start.2 = (bf16[4,32,64]{2,0,1:T(4,128)(2,1)S(1)}, bf16[4,32,64]{2,0,1:T(4,128)(2,1)S(1)}, u32[]{:S(2)}, u32[]{:S(2)}) collective-permute-start(bf16[4,32,64]{2,0,1:T(4,128)(2,1)S(1)} %bitcast.359), channel_id=1, source_target_pairs={{8,0},{0,8},{9,1},{1,9},{10,2},{2,10},{11,3},{3,11},{12,4},{4,12},... | collective-permute-start | bytes 49160 | tf_op jit(solution)/shard_map/ppermute | solution.py:12
  36.1 24.3 %copy-start.1 = (bf16[4,1,4,64,256]{4,3,2,1,0:T(8,128)(2,1)S(1)}, bf16[4,1,4,64,256]{4,3,2,1,0:T(8,128)(2,1)}, u32[]{:S(2)}) copy-start(bf16[4,1,4,64,256]{4,3,2,1,0:T(8,128)(2,1)} %param.31) | copy-start | bytes 1572868
  36.1 30.6 %copy-start.14 = (s32[2,32]{1,0:T(2,128)S(1)}, s32[2,32]{1,0:T(2,128)}, u32[]{:S(2)}) copy-start(s32[2,32]{1,0:T(2,128)} %param.35) | copy-start | bytes 772
  36.2 30.6 %copy-start.15 = (s32[2,32]{1,0:T(2,128)S(1)}, s32[2,32]{1,0:T(2,128)}, u32[]{:S(2)}) copy-start(s32[2,32]{1,0:T(2,128)} %param.34) | copy-start | bytes 772
  58.9 10.3 %copy-start.16 = (s32[4]{0:T(128)S(1)}, s32[4]{0:T(128)}, u32[]{:S(2)}) copy-start(s32[4]{0:T(128)} %constant.340.clone.1) | copy-start | bytes 52
  58.9 13.0 %copy-start.17 = (u32[32]{0:T(128)S(1)}, u32[32]{0:T(128)}, u32[]{:S(2)}) copy-start(u32[32]{0:T(128)} %constant.350) | copy-start | bytes 388
  58.9 16.2 %copy-start = (bf16[4,1,4,64,256]{4,3,2,1,0:T(8,128)(2,1)S(1)}, bf16[4,1,4,64,256]{4,3,2,1,0:T(8,128)(2,1)}, u32[]{:S(2)}) copy-start(bf16[4,1,4,64,256]{4,3,2,1,0:T(8,128)(2,1)} %param.30) | copy-start | bytes 1572868
  59.9 14.3 %collective-permute-start.3 = (bf16[4,32,64]{2,0,1:T(4,128)(2,1)S(1)}, bf16[4,32,64]{2,0,1:T(4,128)(2,1)S(1)}, u32[]{:S(2)}, u32[]{:S(2)}) collective-permute-start(bf16[4,32,64]{2,0,1:T(4,128)(2,1)S(1)} %bitcast.358), channel_id=1, source_target_pairs={{8,0},{0,8},{9,1},{1,9},{10,2},{2,10},{11,3},{3,11},{12,4},{4,12},... | collective-permute-start | bytes 49160 | tf_op jit(solution)/shard_map/ppermute | solution.py:12
  61.2 14.2 %copy-start.12 = (bf16[7,64,64]{2,1,0:T(8,128)(2,1)S(1)}, bf16[7,64,64]{2,1,0:T(8,128)(2,1)}, u32[]{:S(2)}) copy-start(bf16[7,64,64]{2,1,0:T(8,128)(2,1)} %param.32) | copy-start | bytes 172036
  61.2 20.0 %collective-permute-start.1 = (bf16[1,4,64,256]{3,2,1,0:T(8,128)(2,1)}, bf16[1,4,64,256]{3,2,1,0:T(8,128)(2,1)}, u32[]{:S(2)}, u32[]{:S(2)}) collective-permute-start(bf16[1,4,64,256]{3,2,1,0:T(8,128)(2,1)} %get-tuple-element.162), channel_id=1, source_target_pairs={{0,16},{1,17},{2,18},{3,19},{4,20},{5,21},{6,22},{7,23},{8,24},{9,... | collective-permute-start | bytes 393224 | tf_op jit(solution)/shard_map/ppermute | solution.py:22
  65.4 20.6 %collective-permute-start = (bf16[1,4,64,256]{3,2,1,0:T(8,128)(2,1)}, bf16[1,4,64,256]{3,2,1,0:T(8,128)(2,1)}, u32[]{:S(2)}, u32[]{:S(2)}) collective-permute-start(bf16[1,4,64,256]{3,2,1,0:T(8,128)(2,1)} %get-tuple-element.161), channel_id=1, source_target_pairs={{16,0},{17,1},{18,2},{19,3},{20,4},{21,5},{22,6},{23,7},{24,8},{25... | collective-permute-start | bytes 393224 | tf_op jit(solution)/shard_map/ppermute | solution.py:23
  74.2 8.3 %copy-start.7 = (bf16[4,4,64,1]{3,2,1,0:T(8,128)(2,1)}, bf16[4,4,64,1]{3,2,1,0:T(8,128)(2,1)S(1)}, u32[]{:S(2)}) copy-start(bf16[4,4,64,1]{3,2,1,0:T(8,128)(2,1)S(1)} %copy.92) | copy-start | bytes 6148
  75.1 7.4 %copy-start.9 = (bf16[4,4,64,1]{3,2,1,0:T(8,128)(2,1)}, bf16[4,4,64,1]{3,2,1,0:T(8,128)(2,1)S(1)}, u32[]{:S(2)}) copy-start(bf16[4,4,64,1]{3,2,1,0:T(8,128)(2,1)S(1)} %copy.96) | copy-start | bytes 6148
  76.2 5.0 %copy-start.13 = (bf16[3,64,64]{2,1,0:T(8,128)(2,1)S(1)}, bf16[3,64,64]{2,1,0:T(8,128)(2,1)}, u32[]{:S(2)}) copy-start(bf16[3,64,64]{2,1,0:T(8,128)(2,1)} %param.33) | copy-start | bytes 73732
  76.3 6.2 %collective-permute-start.4 = (bf16[4,1,64,258]{3,2,1,0:T(8,128)(2,1)S(1)}, bf16[4,1,64,258]{3,2,1,0:T(8,128)(2,1)S(1)}, u32[]{:S(2)}, u32[]{:S(2)}) collective-permute-start(bf16[4,1,64,258]{3,2,1,0:T(8,128)(2,1)S(1)} %get-tuple-element.159), channel_id=1, source_target_pairs={{1,0},{2,1},{3,2},{4,3},{5,4},{6,5},{7,6},{9,8},{10,9},{11,10},{12... | collective-permute-start | bytes 396296 | tf_op jit(solution)/shard_map/ppermute | solution.py:23
  77.7 4.8 %collective-permute-start.5 = (bf16[4,1,64,258]{3,2,1,0:T(8,128)(2,1)S(1)}, bf16[4,1,64,258]{3,2,1,0:T(8,128)(2,1)S(1)}, u32[]{:S(2)}, u32[]{:S(2)}) collective-permute-start(bf16[4,1,64,258]{3,2,1,0:T(8,128)(2,1)S(1)} %get-tuple-element.160), channel_id=1, source_target_pairs={{0,1},{1,2},{2,3},{3,4},{4,5},{5,6},{6,7},{8,9},{9,10},{10,11},{11... | collective-permute-start | bytes 396296 | tf_op jit(solution)/shard_map/ppermute | solution.py:22
  83.2 1.1 copy-start.3
  83.2 1.3 copy-start.5
  129.9 1.3 copy-start.8
  129.9 2.3 copy-start.10
  131.2 2.0 copy-start.6
  131.2 3.0 copy-start.4
  134.2 2.9 copy-start.2
  137.1 10.3 %copy-start.11 = (bf16[4,4,64,256]{3,2,1,0:T(8,128)(2,1)S(1)}, bf16[4,4,64,256]{3,2,1,0:T(8,128)(2,1)}, u32[]{:S(2)}) copy-start(bf16[4,4,64,256]{3,2,1,0:T(8,128)(2,1)} %get-tuple-element.167) | copy-start | bytes 1572868
  140.4 127.0 %collective-permute-start.6 = (bf16[4,64,258]{2,1,0:T(8,128)(2,1)}, bf16[4,64,258]{2,1,0:T(8,128)(2,1)}, u32[]{:S(2)}, u32[]{:S(2)}) collective-permute-start(bf16[4,64,258]{2,1,0:T(8,128)(2,1)} %get-tuple-element.156), channel_id=1, source_target_pairs={{0,1},{1,2},{2,3},{3,4},{4,5},{5,6},{6,7},{8,9},{9,10},{10,11},{11... | collective-permute-start | bytes 396296 | tf_op jit(solution)/shard_map/ppermute | solution.py:31
  144.8 125.8 %collective-permute-start.7 = (bf16[4,64,258]{2,1,0:T(8,128)(2,1)}, bf16[4,64,258]{2,1,0:T(8,128)(2,1)}, u32[]{:S(2)}, u32[]{:S(2)}) collective-permute-start(bf16[4,64,258]{2,1,0:T(8,128)(2,1)} %get-tuple-element.155), channel_id=1, source_target_pairs={{1,0},{2,1},{3,2},{4,3},{5,4},{6,5},{7,6},{9,8},{10,9},{11,10},{12... | collective-permute-start | bytes 396296 | tf_op jit(solution)/shard_map/ppermute | solution.py:31
  273.0 4.3 %collective-permute-start.8 = (bf16[4,32,64]{2,0,1:T(4,128)(2,1)S(1)}, bf16[4,32,64]{2,0,1:T(4,128)(2,1)S(1)}, u32[]{:S(2)}, u32[]{:S(2)}) collective-permute-start(bf16[4,32,64]{2,0,1:T(4,128)(2,1)S(1)} %convert_element_type.38), channel_id=1, source_target_pairs={{8,0},{0,8},{9,1},{1,9},{10,2},{2,10},{11,3},{3,11},{12,4},{4,12},... | collective-permute-start | bytes 49160 | tf_op jit(solution)/shard_map/ppermute | solution.py:12
  275.2 4.0 %collective-permute-start.9 = (bf16[4,32,64]{2,0,1:T(4,128)(2,1)S(1)}, bf16[4,32,64]{2,0,1:T(4,128)(2,1)S(1)}, u32[]{:S(2)}, u32[]{:S(2)}) collective-permute-start(bf16[4,32,64]{2,0,1:T(4,128)(2,1)S(1)} %convert_element_type.39), channel_id=1, source_target_pairs={{8,0},{0,8},{9,1},{1,9},{10,2},{2,10},{11,3},{3,11},{12,4},{4,12},... | collective-permute-start | bytes 49160 | tf_op jit(solution)/shard_map/ppermute | solution.py:12
Sparse Core Ops, SparseCore 0:
  137.3 128.2 all-reduce.5
where the time goes:
time: 318 us; the launch traced here: 317 us
  blocking collectives  120 us (38%)
  waiting for transfers between devices  74.3 us (23%)
  local copies, waits for them, and re-layouts  49.8 us (16%)
  matrix products  27.6 us (9%)
  starting transfers between devices  20.2 us (6%)
  between operations  15.2 us (5%)
  other arithmetic  9.59 us (3%)
    psum x1, waiting for transfers between devices, shards(): lax.psum((hex_local, time_local), ('tm', 'diamond', 'tile'))  71.3 us
    psum x1, blocking collectives, shards(): lax.psum((hex_local, time_local), ('tm', 'diamond', 'tile'))  45.7 us
    scatter-add x5, local copies, waits for them, and re-layouts, shards(): spread = spread.at[:, 1 + step_row:1 + step_row + tile_rows, :, 1 + step_...  30.8 us
    unnamed x1, blocking collectives  26.9 us
    all_gather x1, blocking collectives, shards(): lax.all_gather(field[..., 0], 'tile', axis=1, tiled=True)  25.1 us
    all_gather x1, blocking collectives, shards(): lax.all_gather(field[..., columns - 1], 'tile', axis=1, tiled=True)  22.7 us
    dot_general x7, matrix products, shards(): jnp.einsum('frdx,cd->frcx', grad_wide, hex_weight[number], preferred_elem...  9.43 us
    ppermute x2, starting transfers between devices, with_halo(): before = lax.ppermute(last, axis, up)  7.4 us
  transfers between devices with their start and end apart: 11, of which 3 were waited for; matrix products, arithmetic and copies ran while one was open for 9% of the time, Pallas kernels for 0%

commit v1 on v0

--- a/solution.py
+++ b/solution.py
@@ -129,7 +129,7 @@
     total = total.at[..., 0].add(into_first)
     hex_local = jnp.stack(hex_terms)
     time_local = jnp.stack(time_terms)
-    grad_hex, grad_time = lax.psum((hex_local, time_local), ("tm", "diamond", "tile"))
+    grad_hex, grad_time = lax.psum(lax.psum((hex_local, time_local), ("diamond", "tile")), "tm")
     return (total.astype(jnp.bfloat16)[:, None], grad_hex, grad_time)
 
 

time: 318 us -> 268 us (0.84)
  waiting for transfers between devices: 74.3 us -> 2.94 us
  blocking collectives: 120 us -> 146 us
  matrix products: 27.6 us -> 22.4 us
    psum x1 -> x2, waiting for transfers between devices: 71.3 us -> 0.01 us  [the longest x1 0.01 us: shards(): lax.psum((hex_local, time_local), ('diamond', 'tile'))]
    psum x1 -> x2, blocking collectives: 45.7 us -> 72.1 us  [the longest x1 60.2 us: shards(): lax.psum((hex_local, time_local), ('diamond', 'tile'))]
    dot_general x7, matrix products: 6.82 us -> 2.47 us  [shards(): jnp.einsum('frcx,frdx->cd', window, grad_wide, preferred_element_type=jnp...]
  transfers between devices with their start and end apart: 11 -> 12, of which waited for: 3 -> 2; matrix products, arithmetic and copies ran while one was open for 9% -> 27% of each run, Pallas kernels for 0% -> 0%
where the time goes in v1:
time: 268 us; the launch traced here: 267 us
  blocking collectives  146 us (54%)
  local copies, waits for them, and re-layouts  50.9 us (19%)
  matrix products  22.4 us (8%)
  starting transfers between devices  20.4 us (8%)
  between operations  15.3 us (6%)
  other arithmetic  8.9 us (3%)
  waiting for transfers between devices  2.94 us (1%)
    psum x1, blocking collectives, shards(): lax.psum((hex_local, time_local), ('diamond', 'tile'))  60.2 us
    scatter-add x5, local copies, waits for them, and re-layouts, shards(): spread = spread.at[:, 1 + step_row:1 + step_row + tile_rows, :, 1 + step_...  32.5 us
    unnamed x1, blocking collectives  26.3 us
    all_gather x1, blocking collectives, shards(): lax.all_gather(field[..., 0], 'tile', axis=1, tiled=True)  25.1 us
    all_gather x1, blocking collectives, shards(): lax.all_gather(field[..., columns - 1], 'tile', axis=1, tiled=True)  22.7 us
    psum x1, blocking collectives, shards(): lax.psum(lax.psum((hex_local, time_local), ('diamond', 'tile')), 'tm')  11.8 us
    dot_general x7, matrix products, shards(): jnp.einsum('frdx,cd->frcx', grad_wide, hex_weight[number], preferred_elem...  9.91 us
    ppermute x2, starting transfers between devices, with_halo(): before = lax.ppermute(last, axis, up)  7.2 us
  transfers between devices with their start and end apart: 12, of which 2 were waited for; matrix products, arithmetic and copies ran while one was open for 27% of the time, Pallas kernels for 0%

profile of v1, /device:TPU:0, one launch (start us, length us, event | category | flops | bytes accessed | tf_op | source)
XLA Modules:
  0.0 267.2 jit_solution(12246628503859750413)
XLA Ops:
  7.2 1.2 fusion.91
  8.4 25.1 %all-gather = bf16[4,32,64,1]{3,2,1,0:T(8,128)(2,1)S(1)} all-gather(bf16[4,4,64,1]{3,2,1,0:T(8,128)(2,1)S(1)} %get-tuple-element.164), channel_id=2, replica_groups=mesh['tm'=2,'diamond'=2,'tile'=8] {'tile'}, dimensions={1}, use_global_device_ids=true | all-gather | bytes 18432 | tf_op jit(solution)/shard_map/all_gather | solution.py:49
  33.5 1.1 copy.161
  34.6 1.6 collective-permute-start.2
  36.1 22.7 %all-gather.1 = bf16[4,32,64,1]{3,2,1,0:T(8,128)(2,1)S(1)} all-gather(bf16[4,4,64,1]{3,2,1,0:T(8,128)(2,1)S(1)} %get-tuple-element.163), channel_id=3, replica_groups=mesh['tm'=2,'diamond'=2,'tile'=8] {'tile'}, dimensions={1}, use_global_device_ids=true | all-gather | bytes 18432 | tf_op jit(solution)/shard_map/all_gather | solution.py:50
  58.9 1.1 copy.162
  60.5 0.7 slice_bitcast_fusion.4
  61.2 4.2 %collective-permute-start.1 = (bf16[1,4,64,256]{3,2,1,0:T(8,128)(2,1)}, bf16[1,4,64,256]{3,2,1,0:T(8,128)(2,1)}, u32[]{:S(2)}, u32[]{:S(2)}) collective-permute-start(bf16[1,4,64,256]{3,2,1,0:T(8,128)(2,1)} %get-tuple-element.162), channel_id=1, source_target_pairs={{0,16},{1,17},{2,18},{3,19},{4,20},{5,21},{6,22},{7,23},{8,24},{9,... | collective-permute-start | bytes 393224 | tf_op jit(solution)/shard_map/ppermute | solution.py:22
  65.4 1.3 collective-permute-start
  66.9 1.0 convolution_bitcast_fusion.16
  69.1 2.5 and_reduce_fusion
  72.2 0.6 dynamic-slice.105
  73.5 1.3 gather_fusion
  77.2 1.4 collective-permute-start.4
  78.6 3.0 %collective-permute-start.5 = (bf16[4,1,64,258]{3,2,1,0:T(8,128)(2,1)S(1)}, bf16[4,1,64,258]{3,2,1,0:T(8,128)(2,1)S(1)}, u32[]{:S(2)}, u32[]{:S(2)}) collective-permute-start(bf16[4,1,64,258]{3,2,1,0:T(8,128)(2,1)S(1)} %get-tuple-element.160), channel_id=1, source_target_pairs={{0,1},{1,2},{2,3},{3,4},{4,5},{5,6},{6,7},{8,9},{9,10},{10,11},{11... | collective-permute-start | bytes 396296 | tf_op jit(solution)/shard_map/ppermute | solution.py:22
  82.0 1.2 convolution_bitcast_fusion.13
  83.2 0.7 pad_maximum_fusion
  85.1 1.5 multiply_convert_fusion
  86.5 1.5 fusion.15
  90.9 0.7 copy-done.6
  92.1 1.4 fusion.9
  93.5 1.7 scatter-add.36
  95.2 7.1 %scatter-add.39 = f32[4,6,64,258]{3,2,0,1:T(8,128)S(1)} dynamic-update-slice(f32[4,6,64,258]{3,2,0,1:T(8,128)S(1)} %scatter-add.36, f32[4,4,64,256]{3,2,0,1:T(8,128)} %fusion.9, s32[]{:T(128)} %constant.332.clone.1, s32[]{:T(128)} %constant.338.clone.1, s32[]{:T(128)} %constant.332.clone.1, s32[]{:T(128)} %constant.333.clone.1) | dynamic-update-slice | bytes 2097156 | tf_op jit(solution)/shard_map/scatter-add | solution.py:93
  102.6 1.3 fusion.12
  103.9 7.1 %scatter-add.41 = f32[4,6,64,258]{3,2,0,1:T(8,128)S(1)} dynamic-update-slice(f32[4,6,64,258]{3,2,0,1:T(8,128)S(1)} %fusion.11, f32[4,4,64,256]{3,2,0,1:T(8,128)} %fusion.12, s32[]{:T(128)} %constant.332.clone.1, s32[]{:T(128)} %constant.333.clone.1, s32[]{:T(128)} %constant.332.clone.1, s32[]{:T(128)} %constant.338.clone.1) | dynamic-update-slice | bytes 2097156 | tf_op jit(solution)/shard_map/scatter-add | solution.py:93
  111.0 3.2 %add_select_fusion.1 = f32[4,4,64,256]{3,2,0,1:T(8,128)} fusion(f32[4,6,64,258]{3,2,0,1:T(8,128)S(1)} %scatter-add.41, s32[]{:T(128)} %bitcast.365, s32[]{:T(128)} %bitcast.61, pred[]{:T(512)} %get-tuple-element.148, bf16[4,4,64,256]{3,2,1,0:T(8,128)(2,1)S(1)} %fusion.15, bf16[7,64,64]{2,1,0:T(8,128)(2,1)S(1)} %copy-done.5), kind=kOutput, calls=%fused_computation.5 | convolution fusion | flops 34078720 | bytes 2637833 | tf_op jit(solution)/shard_map/frdx,cd->frcx/dot_general | solution.py:94
  114.2 8.3 %scatter-add.44 = f32[4,6,64,258]{3,2,0,1:T(8,128)S(1)} dynamic-update-slice(f32[4,6,64,258]{3,2,0,1:T(8,128)S(1)} %scatter-add.41, f32[4,4,64,256]{3,2,0,1:T(8,128)} %add_select_fusion.1, s32[]{:T(128)} %constant.332.clone.1, s32[]{:T(128)} %bitcast.366, s32[]{:T(128)} %constant.332.clone.1, s32[]{:T(128)} %bitcast.61) | dynamic-update-slice | bytes 2097156 | tf_op jit(solution)/shard_map/scatter-add | solution.py:93
  122.8 3.2 %add_select_fusion = f32[4,4,64,256]{3,2,0,1:T(8,128)} fusion(f32[4,6,64,258]{3,2,0,1:T(8,128)S(1)} %fusion.14, s32[]{:T(128)} %bitcast.66, s32[]{:T(128)} %bitcast.67, pred[]{:T(512)} %get-tuple-element.147, bf16[4,4,64,256]{3,2,1,0:T(8,128)(2,1)S(1)} %fusion.15, bf16[7,64,64]{2,1,0:T(8,128)(2,1)S(1)} %copy-done.5), kind=kOutput, calls=%fused_computation.4 | convolution fusion | flops 34078720 | bytes 2637833 | tf_op jit(solution)/shard_map/frdx,cd->frcx/dot_general | solution.py:94
  126.0 8.3 %scatter-add.46 = f32[4,6,64,258]{3,2,0,1:T(8,128)S(1)} dynamic-update-slice(f32[4,6,64,258]{3,2,0,1:T(8,128)S(1)} %fusion.14, f32[4,4,64,256]{3,2,0,1:T(8,128)} %add_select_fusion, s32[]{:T(128)} %constant.332.clone.1, s32[]{:T(128)} %bitcast.66, s32[]{:T(128)} %constant.332.clone.1, s32[]{:T(128)} %bitcast.67) | dynamic-update-slice | bytes 2097156 | tf_op jit(solution)/shard_map/scatter-add | solution.py:93
  134.5 4.6 %collective-permute-start.6 = (bf16[4,64,258]{2,1,0:T(8,128)(2,1)S(1)}, bf16[4,64,258]{2,1,0:T(8,128)(2,1)}, u32[]{:S(2)}, u32[]{:S(2)}) collective-permute-start(bf16[4,64,258]{2,1,0:T(8,128)(2,1)S(1)} %get-tuple-element.156), channel_id=1, source_target_pairs={{0,1},{1,2},{2,3},{3,4},{4,5},{5,6},{6,7},{8,9},{9,10},{10,11},{11... | collective-permute-start | bytes 396296 | tf_op jit(solution)/shard_map/ppermute | solution.py:31
  139.2 1.2 convolution_bitcast_fusion.17
  140.4 1.2 convolution_bitcast_fusion.19
  141.6 60.2 %psum.30 = f32[3,64,64]{2,1,0:T(8,128)S(1)} all-reduce(f32[3,64,64]{2,1,0:T(8,128)S(1)} %pad_maximum_fusion.16), channel_id=1, replica_groups=mesh['tm'=2,'diamond'=2,'tile'=8] {'diamond','tile'}, use_global_device_ids=true, to_apply=%region_8.10 | all-reduce | flops 12288 | bytes 98304 | tf_op jit(solution)/shard_map/psum | solution.py:132
  201.8 1.3 slice.528
  203.1 1.3 collective-permute-start.7
  204.4 11.8 %psum.31 = f32[3,64,64]{2,1,0:T(8,128)} all-reduce(f32[3,64,64]{2,1,0:T(8,128)S(1)} %psum.30), channel_id=1, replica_groups=mesh['tm'=2,'diamond'=2,'tile'=8] {'tm'}, use_global_device_ids=true, to_apply=%region_9.11 | all-reduce | flops 12288 | bytes 98304 | tf_op jit(solution)/shard_map/psum | solution.py:132
  216.3 1.7 fusion.33
  218.0 1.6 copy.119
  219.6 1.1 fusion.32
  221.9 1.4 collective-permute-start.8
  224.0 0.8 collective-permute-start.9
  225.1 1.0 collective-permute-done.8
  226.1 1.9 collective-permute-done.9
  228.0 26.3 %all-reduce.3 = (bf16[4,32,64]{2,0,1:T(4,128)(2,1)S(1)}, bf16[4,32,64]{2,0,1:T(4,128)(2,1)S(1)}) all-reduce(bf16[4,32,64]{2,0,1:T(4,128)(2,1)S(1)} %collective-permute-done.8, bf16[4,32,64]{2,0,1:T(4,128)(2,1)S(1)} %collective-permute-done.9), channel_id=4, replica_groups=mesh['tm'=2,'diamond'=2,'tile'=8] {'tile'}, use_global_device_ids=true, to_apply=%region_3.5.clone | all-reduce | flops 16384 | bytes 65536
  255.1 1.9 scatter-add.51
  257.1 0.6 scatter-add.54
  257.7 0.9 convert_bitcast_fusion
  258.6 1.8 copy.133
  (98 shorter events, 13.5 us)
Async XLA Ops:
  7.2 209.1 %all-reduce.7.cloned.1.call-start = ((), (), s32[]{:S(2)}) async-start(), calls=%async_computation | async-start | bytes 458752 | tf_op jit(solution)/shard_map/psum | solution.py:132
  34.6 38.9 %collective-permute-start.2 = (bf16[4,32,64]{2,0,1:T(4,128)(2,1)S(1)}, bf16[4,32,64]{2,0,1:T(4,128)(2,1)}, u32[]{:S(2)}, u32[]{:S(2)}) collective-permute-start(bf16[4,32,64]{2,0,1:T(4,128)(2,1)S(1)} %bitcast.359), channel_id=1, source_target_pairs={{8,0},{0,8},{9,1},{1,9},{10,2},{2,10},{11,3},{3,11},{12,4},{4,12},... | collective-permute-start | bytes 49160 | tf_op jit(solution)/shard_map/ppermute | solution.py:12
  36.1 24.4 %copy-start.1 = (bf16[4,1,4,64,256]{4,3,2,1,0:T(8,128)(2,1)S(1)}, bf16[4,1,4,64,256]{4,3,2,1,0:T(8,128)(2,1)}, u32[]{:S(2)}) copy-start(bf16[4,1,4,64,256]{4,3,2,1,0:T(8,128)(2,1)} %param.31) | copy-start | bytes 1572868
  58.9 7.9 %copy-start.11 = (s32[2,32]{1,0:T(2,128)S(1)}, s32[2,32]{1,0:T(2,128)}, u32[]{:S(2)}) copy-start(s32[2,32]{1,0:T(2,128)} %param.35) | copy-start | bytes 772
  58.9 8.0 %copy-start.12 = (s32[2,32]{1,0:T(2,128)S(1)}, s32[2,32]{1,0:T(2,128)}, u32[]{:S(2)}) copy-start(s32[2,32]{1,0:T(2,128)} %param.34) | copy-start | bytes 772
  58.9 10.2 %copy-start.13 = (s32[4]{0:T(128)S(1)}, s32[4]{0:T(128)}, u32[]{:S(2)}) copy-start(s32[4]{0:T(128)} %constant.340.clone.1) | copy-start | bytes 52
  58.9 13.3 %copy-start.14 = (u32[32]{0:T(128)S(1)}, u32[32]{0:T(128)}, u32[]{:S(2)}) copy-start(u32[32]{0:T(128)} %constant.350) | copy-start | bytes 388
  58.9 17.2 %copy-start = (bf16[4,1,4,64,256]{4,3,2,1,0:T(8,128)(2,1)S(1)}, bf16[4,1,4,64,256]{4,3,2,1,0:T(8,128)(2,1)}, u32[]{:S(2)}) copy-start(bf16[4,1,4,64,256]{4,3,2,1,0:T(8,128)(2,1)} %param.30) | copy-start | bytes 1572868
  59.9 15.2 %collective-permute-start.3 = (bf16[4,32,64]{2,0,1:T(4,128)(2,1)S(1)}, bf16[4,32,64]{2,0,1:T(4,128)(2,1)S(1)}, u32[]{:S(2)}, u32[]{:S(2)}) collective-permute-start(bf16[4,32,64]{2,0,1:T(4,128)(2,1)S(1)} %bitcast.358), channel_id=1, source_target_pairs={{8,0},{0,8},{9,1},{1,9},{10,2},{2,10},{11,3},{3,11},{12,4},{4,12},... | collective-permute-start | bytes 49160 | tf_op jit(solution)/shard_map/ppermute | solution.py:12
  61.2 15.1 %copy-start.5 = (bf16[7,64,64]{2,1,0:T(8,128)(2,1)S(1)}, bf16[7,64,64]{2,1,0:T(8,128)(2,1)}, u32[]{:S(2)}) copy-start(bf16[7,64,64]{2,1,0:T(8,128)(2,1)} %param.32) | copy-start | bytes 172036
  61.2 20.8 %collective-permute-start.1 = (bf16[1,4,64,256]{3,2,1,0:T(8,128)(2,1)}, bf16[1,4,64,256]{3,2,1,0:T(8,128)(2,1)}, u32[]{:S(2)}, u32[]{:S(2)}) collective-permute-start(bf16[1,4,64,256]{3,2,1,0:T(8,128)(2,1)} %get-tuple-element.162), channel_id=1, source_target_pairs={{0,16},{1,17},{2,18},{3,19},{4,20},{5,21},{6,22},{7,23},{8,24},{9,... | collective-permute-start | bytes 393224 | tf_op jit(solution)/shard_map/ppermute | solution.py:22
  65.4 21.1 %collective-permute-start = (bf16[1,4,64,256]{3,2,1,0:T(8,128)(2,1)}, bf16[1,4,64,256]{3,2,1,0:T(8,128)(2,1)}, u32[]{:S(2)}, u32[]{:S(2)}) collective-permute-start(bf16[1,4,64,256]{3,2,1,0:T(8,128)(2,1)} %get-tuple-element.161), channel_id=1, source_target_pairs={{16,0},{17,1},{18,2},{19,3},{20,4},{21,5},{22,6},{23,7},{24,8},{25... | collective-permute-start | bytes 393224 | tf_op jit(solution)/shard_map/ppermute | solution.py:23
  69.1 4.4 %copy-start.8 = (s32[2]{0:T(128)}, s32[2]{0:T(128)S(1)}, u32[]{:S(2)}) copy-start(s32[2]{0:T(128)S(1)} %iota.16) | copy-start | bytes 28
  77.2 4.8 %copy-start.7 = (bf16[3,64,64]{2,1,0:T(8,128)(2,1)S(1)}, bf16[3,64,64]{2,1,0:T(8,128)(2,1)}, u32[]{:S(2)}) copy-start(bf16[3,64,64]{2,1,0:T(8,128)(2,1)} %param.33) | copy-start | bytes 73732
  77.2 6.0 %collective-permute-start.4 = (bf16[4,1,64,258]{3,2,1,0:T(8,128)(2,1)S(1)}, bf16[4,1,64,258]{3,2,1,0:T(8,128)(2,1)S(1)}, u32[]{:S(2)}, u32[]{:S(2)}) collective-permute-start(bf16[4,1,64,258]{3,2,1,0:T(8,128)(2,1)S(1)} %get-tuple-element.159), channel_id=1, source_target_pairs={{1,0},{2,1},{3,2},{4,3},{5,4},{6,5},{7,6},{9,8},{10,9},{11,10},{12... | collective-permute-start | bytes 396296 | tf_op jit(solution)/shard_map/ppermute | solution.py:23
  78.6 4.6 %collective-permute-start.5 = (bf16[4,1,64,258]{3,2,1,0:T(8,128)(2,1)S(1)}, bf16[4,1,64,258]{3,2,1,0:T(8,128)(2,1)S(1)}, u32[]{:S(2)}, u32[]{:S(2)}) collective-permute-start(bf16[4,1,64,258]{3,2,1,0:T(8,128)(2,1)S(1)} %get-tuple-element.160), channel_id=1, source_target_pairs={{0,1},{1,2},{2,3},{3,4},{4,5},{5,6},{6,7},{8,9},{9,10},{10,11},{11... | collective-permute-start | bytes 396296 | tf_op jit(solution)/shard_map/ppermute | solution.py:22
  88.6 3.5 %copy-start.2 = (f32[4,4,64,256]{3,2,0,1:T(8,128)}, f32[4,4,64,256]{3,2,0,1:T(8,128)S(1)}, u32[]{:S(2)}) copy-start(f32[4,4,64,256]{3,2,0,1:T(8,128)S(1)} %convolution_bitcast_fusion.6) | copy-start | bytes 3145732
  89.8 2.0 copy-start.3
  90.8 0.7 copy-start.6
  91.6 167.0 %all-reduce.9.cloned.1.call-start = ((), (), s32[]{:S(2)}) async-start(), calls=%async_computation.1 | async-start | bytes 458752 | tf_op jit(solution)/shard_map/psum | solution.py:132
  134.3 4.9 %copy-start.4 = (bf16[4,4,64,256]{3,2,1,0:T(8,128)(2,1)S(1)}, bf16[4,4,64,256]{3,2,1,0:T(8,128)(2,1)}, u32[]{:S(2)}) copy-start(bf16[4,4,64,256]{3,2,1,0:T(8,128)(2,1)} %get-tuple-element.167) | copy-start | bytes 1572868
  134.5 81.7 %collective-permute-start.6 = (bf16[4,64,258]{2,1,0:T(8,128)(2,1)S(1)}, bf16[4,64,258]{2,1,0:T(8,128)(2,1)}, u32[]{:S(2)}, u32[]{:S(2)}) collective-permute-start(bf16[4,64,258]{2,1,0:T(8,128)(2,1)S(1)} %get-tuple-element.156), channel_id=1, source_target_pairs={{0,1},{1,2},{2,3},{3,4},{4,5},{5,6},{6,7},{8,9},{9,10},{10,11},{11... | collective-permute-start | bytes 396296 | tf_op jit(solution)/shard_map/ppermute | solution.py:31
  203.1 16.5 %collective-permute-start.7 = (bf16[4,64,258]{2,1,0:T(8,128)(2,1)S(1)}, bf16[4,64,258]{2,1,0:T(8,128)(2,1)}, u32[]{:S(2)}, u32[]{:S(2)}) collective-permute-start(bf16[4,64,258]{2,1,0:T(8,128)(2,1)S(1)} %get-tuple-element.155), channel_id=1, source_target_pairs={{1,0},{2,1},{3,2},{4,3},{5,4},{6,5},{7,6},{9,8},{10,9},{11,10},{12... | collective-permute-start | bytes 396296 | tf_op jit(solution)/shard_map/ppermute | solution.py:31
  218.0 3.3 %copy-start.10 = (s32[4]{0:T(128)S(1)}, s32[4]{0:T(128)}, u32[]{:S(2)}) copy-start(s32[4]{0:T(128)} %get-tuple-element.169) | copy-start | bytes 52
  218.0 5.4 %copy-start.9 = (s32[4]{0:T(128)S(1)}, s32[4]{0:T(128)}, u32[]{:S(2)}) copy-start(s32[4]{0:T(128)} %get-tuple-element.170) | copy-start | bytes 52
  221.9 4.2 %collective-permute-start.8 = (bf16[4,32,64]{2,0,1:T(4,128)(2,1)S(1)}, bf16[4,32,64]{2,0,1:T(4,128)(2,1)S(1)}, u32[]{:S(2)}, u32[]{:S(2)}) collective-permute-start(bf16[4,32,64]{2,0,1:T(4,128)(2,1)S(1)} %convert_element_type.38), channel_id=1, source_target_pairs={{8,0},{0,8},{9,1},{1,9},{10,2},{2,10},{11,3},{3,11},{12,4},{4,12},... | collective-permute-start | bytes 49160 | tf_op jit(solution)/shard_map/ppermute | solution.py:12
  224.0 4.0 %collective-permute-start.9 = (bf16[4,32,64]{2,0,1:T(4,128)(2,1)S(1)}, bf16[4,32,64]{2,0,1:T(4,128)(2,1)S(1)}, u32[]{:S(2)}, u32[]{:S(2)}) collective-permute-start(bf16[4,32,64]{2,0,1:T(4,128)(2,1)S(1)} %convert_element_type.39), channel_id=1, source_target_pairs={{8,0},{0,8},{9,1},{1,9},{10,2},{2,10},{11,3},{3,11},{12,4},{4,12},... | collective-permute-start | bytes 49160 | tf_op jit(solution)/shard_map/ppermute | solution.py:12
Sparse Core Ops, SparseCore 0:
  91.7 93.8 all-reduce.6
  216.4 19.8 all-reduce.8
